TPU v7x, 128 devices: a whole 4x4x4 slice. The times are simulated.
128 devices in a mesh: side: 2 (over z_lo), group: 2 (over z_hi), shard: 32 (over x, y, core).
Axes of the slice: x: 4, y: 4, z: 4 (z_hi: 2, z_lo: 2; z = z_hi * 2 + z_lo), core: 2. Of those that a mesh axis runs over, the one named last changes fastest.
Arguments:
- grad_parts: bfloat16 [4, 4, 7168, 2048], P(('side', 'group'), None, 'shard'), may hold values from -6 to 6
- master: float32 [4, 7168, 2048], P(('side', 'group'), 'shard'), may hold values from -6 to 6
- moment: float32 [4, 7168, 2048], P(('side', 'group'), 'shard'), may hold values from -4 to 4
- variance: float32 [4, 7168, 2048], P(('side', 'group'), 'shard'), may hold values from 0.0004 to 0.04
- plan: int32 [4], replicated, may hold values from 0 to 3, each once
- step: int32 [4], replicated, may hold values from 1 to 16
Outputs:
- new_master: float32 [4, 7168, 2048], P(('side', 'group'), 'shard')
- new_moment: float32 [4, 7168, 2048], P(('side', 'group'), 'shard')
- new_variance: float32 [4, 7168, 2048], P(('side', 'group'), 'shard')
- rollout_weights: bfloat16 [4, 2048, 7168], P(None, 'shard')
Inputs may be any that keep to these rules, and one draw needn't show every extreme that they name: `plan`: a permutation of the slots; slot s belongs to owner group s (groups numbered side-major).
All inputs are finite; a program needn't handle non-finite values.
Results may differ from a plain program's by a relative error of at most 0.0075.
Values may be sent and summed in bfloat16 or wider, within the bound.
A program may use at most 128 MiB of HBM per device.

v0:
```python
import jax
import jax.numpy as jnp
from jax import lax
from jax.sharding import PartitionSpec as P

BETA_ONE = 0.9
BETA_TWO = 0.999
LEARN = 0.1
DECAY = 0.1
EPSILON = 1e-08


def from_root(shard, axis, root):
    mine = lax.axis_index(axis) == root
    return lax.psum(jnp.where(mine, shard, jnp.zeros_like(shard)), axis)


def spread(local, plan, total):
    owned = local.shape[0]
    start = jnp.zeros((total,) + local.shape[1:], local.dtype)

    def one_matrix(index, result):
        slot = plan[index]
        root = slot // owned
        piece = lax.dynamic_index_in_dim(local, slot % owned, 0, keepdims=False)
        got = from_root(piece, ("side", "group"), root)
        return lax.dynamic_update_index_in_dim(result, got, index, 0)

    return lax.fori_loop(0, total, one_matrix, start)


def body(grad_parts, master, moment, variance, plan, step):
    total = plan.shape[0]
    owned = master.shape[0]
    counting = jnp.arange(total, dtype=jnp.int32)
    matching = plan[None, :] == counting[:, None]
    matrix_of_slot = jnp.sum(jnp.where(matching, counting[None, :], 0), axis=1)
    ordered = jnp.take(grad_parts[0], matrix_of_slot, axis=0)
    slotted = lax.psum_scatter(ordered, ("side", "group"), scatter_dimension=0, tiled=True).astype(
        jnp.float32
    )
    new_moment = BETA_ONE * moment + (1.0 - BETA_ONE) * slotted
    new_variance = BETA_TWO * variance + (1.0 - BETA_TWO) * slotted * slotted
    my_slots = lax.axis_index(("side", "group")) * owned + jnp.arange(owned, dtype=jnp.int32)
    my_matrices = jnp.take(matrix_of_slot, my_slots, axis=0)
    count = jnp.take(step, my_matrices, axis=0).astype(jnp.float32)[:, None, None]
    first_fix = 1.0 - jnp.power(jnp.float32(BETA_ONE), count)
    second_fix = 1.0 - jnp.power(jnp.float32(BETA_TWO), count)
    update = new_moment / first_fix / (jnp.sqrt(new_variance / second_fix) + EPSILON)
    new_master = master - LEARN * (update + DECAY * master)
    rounded = new_master.astype(jnp.bfloat16)
    rows_all = spread(rounded, plan, total)
    flipped = jnp.swapaxes(rows_all, 1, 2)
    rollout_weights = lax.all_to_all(flipped, "shard", split_axis=1, concat_axis=2, tiled=True)
    return (new_master, new_moment, new_variance, rollout_weights)


def solution(mesh):
    return jax.shard_map(
        body,
        mesh=mesh,
        in_specs=(
            P(("side", "group"), None, "shard", None),
            P(("side", "group"), "shard", None),
            P(("side", "group"), "shard", None),
            P(("side", "group"), "shard", None),
            P(),
            P(),
        ),
        out_specs=(
            P(("side", "group"), "shard", None),
            P(("side", "group"), "shard", None),
            P(("side", "group"), "shard", None),
            P(None, "shard", None),
        ),
        check_vma=False,
    )
```

profile of v0, /device:TPU:1, one launch (start us, length us, event | category | flops | bytes accessed | tf_op | source)
XLA Modules:
  0.0 390.4 jit_solution(12581636103675443658)
XLA Ops:
  7.2 0.0 reduce-scatter.2.cloned.1.call-start
  7.2 0.8 select_reduce_fusion
  8.0 4.7 %gather_fusion = bf16[4,224,2048]{2,1,0:T(8,128)(2,1)} fusion(bf16[4,224,2048]{2,1,0:T(8,128)(2,1)} %bitcast.21, s32[1024]{0:T(1024)S(1)} %pad_clamp_fusion), kind=kCustom, calls=%fused_computation | custom fusion | bytes 7340048 | tf_op jit(solution)/shard_map/jit(_take)/gather | solution.py:38
  12.7 4.3 %broadcast_select_fusion.1 = bf16[4,224,2048]{2,1,0:T(8,128)(2,1)} fusion(bf16[4,224,2048]{2,1,0:T(8,128)(2,1)} %gather_fusion, pred[4]{0:T(512)(128)(4,1)S(1)} %compare_and_fusion), kind=kLoop, calls=%fused_computation.3 | loop fusion | flops 1835008 | bytes 7340036 | tf_op jit(solution)/shard_map/jit(_take)/select_n | solution.py:38
  17.0 0.0 copy-start.1
  17.0 0.0 copy-start
  17.0 0.0 reduce-scatter.2.cloned.1.call-update
  17.0 0.6 dynamic-slice.4
  18.3 0.0 copy-done.1
  18.3 0.6 dynamic-slice.5
  19.6 73.1 %reduce-scatter.2.cloned.1.call-done = bf16[1,224,2048]{2,1,0:T(8,128)(2,1)} async-done(((bf16[4,224,2048]{2,1,0:T(8,128)(2,1)}), bf16[1,224,2048]{2,1,0:T(8,128)(2,1)}) %reduce-scatter.2.cloned.1.call-update) | async-done | bytes 917520 | tf_op jit(solution)/shard_map/reduce_scatter | solution.py:39
  92.7 0.0 copy-done
  92.7 0.0 copy-start.2
  92.7 5.8 %fusion.3 = (bf16[1,224,2048]{2,1,0:T(8,128)(2,1)S(1)}, f32[1,224,2048]{2,1,0:T(8,128)}, f32[1,224,2048]{2,1,0:T(8,128)}, f32[1,224,2048]{2,1,0:T(8,128)}) fusion(f32[1,224,2048]{2,1,0:T(8,128)S(1)} %copy-done, f32[]{:T(128)} %bitcast.8, f32[]{:T(128)} %bitcast.7, bf16[1,224,2048]{2,1,0:T(8,128)(2,1)} %reduce-scatter.2.cloned.1.call-done, ...), kind=kLoop, calls=%fused_computation.16 | loop fusion | flops 7798784 | bytes 12845064 | tf_op jit(solution)/shard_map/convert_element_type | solution.py:51
  98.5 0.0 copy-done.2
  98.5 204.2 %while.17 = (s32[]{:T(128)}, bf16[4,224,2048]{2,1,0:T(8,128)(2,1)}, s32[4]{0:T(128)S(1)}, bf16[1,224,2048]{2,1,0:T(8,128)(2,1)S(1)}, s32[]{:T(128)}, /*index=5*/u32[]{:T(128)}, u32[]{:T(128)}, u32[]{:T(128)}, s32[]{:T(128)}) while((s32[]{:T(128)}, bf16[4,224,2048]{2,1,0:T(8,128)(2,1)}, s32[4]{0:T(128)S(1)}, ...), condition=%wide.region_4.5_spmd, body=%wide.region_2.4_spmd.sunk | while | flops 917515 | bytes 9175295 | solution.py:29
  98.5 0.0 all-reduce.2.cloned.1.call-start
  98.5 0.6 dynamic_slice.15
  99.7 1.0 broadcast_select_fusion.3
  100.7 0.0 all-reduce.2.cloned.1.call-update
  100.7 43.6 %all-reduce.2.cloned.1.call-done = bf16[1,224,2048]{2,1,0:T(8,128)(2,1)} async-done(((bf16[1,224,2048]{2,1,0:T(8,128)(2,1)}), bf16[1,224,2048]{2,1,0:T(8,128)(2,1)}) %all-reduce.2.cloned.1.call-update) | async-done | bytes 917520 | tf_op jit(solution)/shard_map/while/body/eval_jaxpr/psum | solution.py:15
  144.3 2.2 constant_dynamic-update-slice_fusion.2
  146.5 0.0 all-reduce.2.cloned.1.call-start
  146.5 0.6 dynamic_slice.15
  147.8 1.0 broadcast_select_fusion.3
  148.8 0.0 all-reduce.2.cloned.1.call-update
  148.8 47.8 %all-reduce.2.cloned.1.call-done = bf16[1,224,2048]{2,1,0:T(8,128)(2,1)} async-done(((bf16[1,224,2048]{2,1,0:T(8,128)(2,1)}), bf16[1,224,2048]{2,1,0:T(8,128)(2,1)}) %all-reduce.2.cloned.1.call-update) | async-done | bytes 917520 | tf_op jit(solution)/shard_map/while/body/eval_jaxpr/psum | solution.py:15
  196.6 2.2 constant_dynamic-update-slice_fusion.2
  198.8 0.0 all-reduce.2.cloned.1.call-start
  198.8 0.6 dynamic_slice.15
  200.0 1.0 broadcast_select_fusion.3
  201.0 0.0 all-reduce.2.cloned.1.call-update
  201.1 47.5 %all-reduce.2.cloned.1.call-done = bf16[1,224,2048]{2,1,0:T(8,128)(2,1)} async-done(((bf16[1,224,2048]{2,1,0:T(8,128)(2,1)}), bf16[1,224,2048]{2,1,0:T(8,128)(2,1)}) %all-reduce.2.cloned.1.call-update) | async-done | bytes 917520 | tf_op jit(solution)/shard_map/while/body/eval_jaxpr/psum | solution.py:15
  248.5 2.2 constant_dynamic-update-slice_fusion.2
  250.8 0.0 all-reduce.2.cloned.1.call-start
  250.8 0.6 dynamic_slice.15
  252.0 1.0 broadcast_select_fusion.3
  253.0 0.0 all-reduce.2.cloned.1.call-update
  253.0 47.5 %all-reduce.2.cloned.1.call-done = bf16[1,224,2048]{2,1,0:T(8,128)(2,1)} async-done(((bf16[1,224,2048]{2,1,0:T(8,128)(2,1)}), bf16[1,224,2048]{2,1,0:T(8,128)(2,1)}) %all-reduce.2.cloned.1.call-update) | async-done | bytes 917520 | tf_op jit(solution)/shard_map/while/body/eval_jaxpr/psum | solution.py:15
  300.5 2.2 constant_dynamic-update-slice_fusion.2
  302.7 7.3 %copy.17 = bf16[4,224,2048]{1,0,2:T(4,128)(2,1)} copy(bf16[4,224,2048]{2,1,0:T(8,128)(2,1)} %get-tuple-element.116) | data formatting | bytes 7340032 | tf_op jit(solution)/shard_map/while | solution.py:29
  310.0 60.1 %all_to_all.18 = bf16[4,2048,224]{2,0,1:T(4,128)(2,1)S(1)} all-to-all(bf16[4,2048,224]{2,0,1:T(4,128)(2,1)} %bitcast.20), channel_id=1, replica_groups=mesh['side'=2,'group'=2,'shard'=32] {'shard'}, dimensions={1} | all-to-all | bytes 7340032 | tf_op jit(solution)/shard_map/all_to_all | solution.py:54
  370.1 0.5 copy.18
  370.6 4.4 %copy.19 = bf16[4,64,32,224]{3,2,1,0:T(8,128)(2,1)} copy(bf16[4,64,32,224]{3,1,2,0:T(8,128)(2,1)S(1)} %bitcast.19) | data formatting | bytes 7340032 | tf_op jit(solution)/shard_map/all_to_all | solution.py:54
  375.0 8.8 %all_to_all.16 = bf16[4,64,7168]{2,1,0:T(8,128)(2,1)} reshape(bf16[4,64,32,224]{3,2,1,0:T(8,128)(2,1)} %copy.19) | data formatting | bytes 7340032 | tf_op jit(solution)/shard_map/all_to_all | solution.py:54
  (4 shorter events, 0.0 us)
Async XLA Ops:
  7.2 85.5 %reduce-scatter.2.cloned.1.call-start = ((), (), s32[]{:S(2)}) async-start(), calls=%async_computation.2 | async-start | bytes 4587520 | tf_op jit(solution)/shard_map/reduce_scatter | solution.py:39
  17.0 1.3 copy-start.1
  17.0 75.7 %copy-start = (f32[1,224,2048]{2,1,0:T(8,128)S(1)}, f32[1,224,2048]{2,1,0:T(8,128)}, u32[]{:S(2)}) copy-start(f32[1,224,2048]{2,1,0:T(8,128)} %param.9) | copy-start | bytes 5505028
  92.7 5.8 %copy-start.2 = (s32[4]{0:T(128)S(1)}, s32[4]{0:T(128)}, u32[]{:S(2)}) copy-start(s32[4]{0:T(128)} %param.12) | copy-start | bytes 52
  98.5 45.9 %all-reduce.2.cloned.1.call-start = ((), (), s32[]{:S(2)}) async-start(), calls=%async_computation.3 | async-start | bytes 1835008 | tf_op jit(solution)/shard_map/while/body/eval_jaxpr/psum | solution.py:15
  146.5 50.0 %all-reduce.2.cloned.1.call-start = ((), (), s32[]{:S(2)}) async-start(), calls=%async_computation.3 | async-start | bytes 1835008 | tf_op jit(solution)/shard_map/while/body/eval_jaxpr/psum | solution.py:15
  198.8 49.7 %all-reduce.2.cloned.1.call-start = ((), (), s32[]{:S(2)}) async-start(), calls=%async_computation.3 | async-start | bytes 1835008 | tf_op jit(solution)/shard_map/while/body/eval_jaxpr/psum | solution.py:15
  250.8 49.7 %all-reduce.2.cloned.1.call-start = ((), (), s32[]{:S(2)}) async-start(), calls=%async_computation.3 | async-start | bytes 1835008 | tf_op jit(solution)/shard_map/while/body/eval_jaxpr/psum | solution.py:15
Sparse Core Ops, SparseCore 0:
  17.1 75.5 reduce-scatter.1
  102.2 42.0 all-reduce.1
  150.3 46.2 all-reduce.1
  202.2 46.2 all-reduce.1
  254.2 46.2 all-reduce.1
where the time goes:
time: 391 us; the launch traced here: 390 us
  waiting for transfers between devices  260 us (66%)
  blocking collectives  60.1 us (15%)
  local copies, waits for them, and re-layouts  38 us (10%)
  between operations  15.2 us (4%)
  other arithmetic  14.8 us (4%)
    psum x4, waiting for transfers between devices, from_root(): return lax.psum(jnp.where(mine, shard, jnp.zeros_like(shard)), axis)  186 us
    reduce_scatter x1, waiting for transfers between devices, body(): lax.psum_scatter(ordered, ('side', 'group'), scatter_dimension=0, tiled=T...  73.1 us
    all_to_all x1, blocking collectives, body(): lax.all_to_all(flipped, 'shard', split_axis=1, concat_axis=2, tiled=True)  60.1 us
    all_to_all x3, local copies, waits for them, and re-layouts, body(): lax.all_to_all(flipped, 'shard', split_axis=1, concat_axis=2, tiled=True)  13.7 us
    dynamic_update_slice x4, local copies, waits for them, and re-layouts, one_matrix(): return lax.dynamic_update_index_in_dim(result, got, index, 0)  8.84 us
  transfers between devices with their start and end apart: 5, of which 5 were waited for; matrix products, arithmetic and copies ran while one was open for 0% of the time, Pallas kernels for 0%

commit v1 on v0

v1 whole, which is shorter than its diff:
```python
import functools

import jax
import jax.numpy as jnp
from jax import lax
from jax.experimental import pallas as pl
from jax.experimental.pallas import tpu as pltpu
from jax.sharding import PartitionSpec as P

BETA_ONE = 0.9
BETA_TWO = 0.999
LEARN = 0.1
DECAY = 0.1
EPSILON = 1e-08

ROWS = 224
COLS = 2048
HALF = COLS // 2
PIECE = 32
STEPS = ROWS // PIECE
WIDE = 64
LANE = 128
SHARDS = 32
NB = 4
MERGED = 24
MSG = 4
AHEAD = 2
MESH = pl.DeviceIdType.MESH
BF16 = jnp.bfloat16
F32 = jnp.float32


def power(base, count):
    result = jnp.float32(1.0)
    square = base
    for bit in range(5):
        factor = jnp.where((count & (1 << bit)) != 0, jnp.float32(square), jnp.float32(1.0))
        result = result * factor
        square = square * square
    return result


def main_kernel(
    plan, step, grad_hbm, master_hbm, moment_hbm, variance_hbm,
    new_master, new_moment, new_variance, rollout,
    grad, master, moment, variance,
    to_opposite, to_right, to_left, relay_left, relay_right, from_left, from_right,
    turned, parts, whole, mixed,
    load_sem, s_sem, relay_sem, raw_sem, sum_sem, s_raw_sem, s_sum_sem,
    x_send, x_recv, g_send, g_recv,
):
    side, group, shard = lax.axis_index("side"), lax.axis_index("group"), lax.axis_index("shard")
    z = group * 2 + side
    turn = lax.rem(shard, 4)

    def place(other_z, other_shard):
        return (lax.rem(other_z, 2), other_z // 2, other_shard)

    def slot_of(other_z):
        return lax.rem(other_z, 2) * 2 + other_z // 2

    z_right, z_left, z_far = lax.rem(z + 1, 4), lax.rem(z + 3, 4), lax.rem(z + 2, 4)
    right, left = place(z_right, shard), place(z_left, shard)
    mine, slot_right, slot_left, slot_far = slot_of(z), slot_of(z_right), slot_of(z_left), slot_of(z_far)

    loads = [
        pltpu.make_async_copy(grad_hbm, grad, load_sem.at[0]),
        pltpu.make_async_copy(master_hbm, master, load_sem.at[1]),
        pltpu.make_async_copy(moment_hbm, moment, load_sem.at[2]),
        pltpu.make_async_copy(variance_hbm, variance, load_sem.at[3]),
    ]
    for load in loads:
        load.start()

    barrier = pltpu.get_barrier_semaphore()
    pl.semaphore_signal(barrier, inc=1, device_id=right, device_id_type=MESH)
    pl.semaphore_signal(barrier, inc=1, device_id=left, device_id_type=MESH)

    def greet(offset, carry):
        other = lax.rem(shard + offset, SHARDS)
        pl.semaphore_signal(barrier, inc=1, device_id=place(z, other), device_id_type=MESH)
        return carry

    lax.fori_loop(1, SHARDS, greet, 0)

    def matrix_of(slot):
        found = jnp.int32(0)
        for b in range(1, NB):
            found = jnp.where(plan[b] == slot, jnp.int32(b), found)
        return found

    b_mine, b_right, b_left, b_far = matrix_of(mine), matrix_of(slot_right), matrix_of(slot_left), matrix_of(slot_far)
    count = step[b_mine]
    one = jnp.ones((1, LANE), F32)
    first_scale = one / (one * (1.0 - power(BETA_ONE, count)))
    second_scale = one / (one * (1.0 - power(BETA_TWO, count)))

    loads[0].wait()
    pl.semaphore_wait(barrier, SHARDS + 1)

    def rows_at(position):
        segment = lax.rem(turn + position, 8)
        return pl.multiple_of(jnp.minimum(segment, STEPS - 1) * PIECE, PIECE)

    def rows_of(index):
        position = index + jnp.where(index >= STEPS - turn, 1, 0)
        return pl.ds(rows_at(position), PIECE)

    low, high = pl.ds(0, HALF), pl.ds(HALF, HALF)

    def remote(src, dst, send, recv, where):
        return pltpu.make_async_remote_copy(
            src_ref=src, dst_ref=dst, send_sem=send, recv_sem=recv, device_id=where, device_id_type=MESH
        )

    def relays(i):
        rows = rows_of(i)
        return (
            remote(to_opposite.at[rows, low], relay_left.at[rows, :], s_sem.at[i, 0], relay_sem.at[i, 0], right),
            remote(to_opposite.at[rows, high], relay_right.at[rows, :], s_sem.at[i, 1], relay_sem.at[i, 1], left),
        )

    def raws(i):
        rows = rows_of(i)
        return (
            remote(to_right.at[rows, high], from_left.at[rows, high], s_raw_sem.at[i, 0], raw_sem.at[i, 0], right),
            remote(to_left.at[rows, low], from_right.at[rows, low], s_raw_sem.at[i, 1], raw_sem.at[i, 1], left),
        )

    def sums(i):
        rows = rows_of(i)
        return (
            remote(to_right.at[rows, low], from_left.at[rows, low], s_sum_sem.at[i, 0], sum_sem.at[i, 0], right),
            remote(to_left.at[rows, high], from_right.at[rows, high], s_sum_sem.at[i, 1], sum_sem.at[i, 1], left),
        )

    def begin(i):
        rows = rows_of(i)
        to_opposite[rows, :] = grad[b_far, rows, :]
        to_right[rows, high] = grad[b_right, rows, high]
        to_left[rows, low] = grad[b_left, rows, low]
        for copy in relays(i) + raws(i):
            copy.start()

    def add(i):
        rows = rows_of(i)
        first, second = relays(i)
        to_r, to_l = sums(i)
        first.wait_recv()
        own = grad[b_right, rows, low].astype(F32)
        to_right[rows, low] = (relay_left[rows, :].astype(F32) + own).astype(BF16)
        to_r.start()
        second.wait_recv()
        own = grad[b_left, rows, high].astype(F32)
        to_left[rows, high] = (relay_right[rows, :].astype(F32) + own).astype(BF16)
        to_l.start()

    def update(i):
        rows = rows_of(i)
        for copy in raws(i) + sums(i):
            copy.wait_recv()

        def tile(j, carry):
            lanes = pl.ds(pl.multiple_of(j * LANE, LANE), LANE)
            total = (
                grad[b_mine, rows, lanes].astype(F32)
                + from_left[rows, lanes].astype(F32)
                + from_right[rows, lanes].astype(F32)
            )
            first = BETA_ONE * moment[rows, lanes] + (1.0 - BETA_ONE) * total
            second = BETA_TWO * variance[rows, lanes] + (1.0 - BETA_TWO) * total * total
            old = master[rows, lanes]
            change = (first * first_scale) / (jnp.sqrt(second * second_scale) + EPSILON)
            new_moment[rows, lanes] = first
            new_variance[rows, lanes] = second
            new_master[rows, lanes] = old - LEARN * (change + DECAY * old)
            return carry

        lax.fori_loop(0, COLS // LANE, tile, 0)

    def exchange(phase, landing):
        my_chip, core = shard // 2, lax.rem(shard, 2)

        def turn_chip(chip):
            lanes = pl.ds(pl.multiple_of(chip * LANE, LANE), LANE)
            block = jnp.concatenate(
                [new_master[pl.ds(rows_at(4 * phase + q), PIECE), lanes] for q in range(4)], axis=0
            )
            turned[phase, pl.ds(pl.multiple_of(chip * LANE, LANE), LANE), :] = block.T.astype(BF16)

        def source(other):
            return turned.at[phase, pl.ds(pl.multiple_of(other * WIDE, WIDE), WIDE), :]

        def send(other):
            remote(source(other), landing(shard), x_send.at[phase], x_recv.at[phase], place(z, other)).start()

        turn_chip(my_chip)

        def one(k, carry):
            turn_chip(lax.rem(my_chip + k, SHARDS // 2))

            @pl.when(k > 1)
            def _():
                before = lax.rem(my_chip + k - 1, SHARDS // 2)
                send(before * 2)
                send(before * 2 + 1)

            return carry

        lax.fori_loop(1, SHARDS // 2, one, 0)
        last = lax.rem(my_chip + SHARDS // 2 - 1, SHARDS // 2)
        send(last * 2)
        send(last * 2 + 1)
        send(my_chip * 2 + 1 - core)
        landing(shard)[...] = turned[phase, pl.ds(pl.multiple_of(shard * WIDE, WIDE), WIDE), :]

    def exchanged(phase, landing):
        everything = landing(pl.ds(0, SHARDS - 1))
        remote(everything, everything, x_send.at[phase], x_recv.at[phase], right).wait_recv()

    def gather_copies(phase, buffer, size, slot, way, m, kind):
        where = right if way == 0 else left
        part = buffer.at[slot, pl.ds(m * size, size)]
        return remote(part, part, g_send.at[phase, kind, way, m], g_recv.at[phase, kind, way, m], where)

    ORDER = ((0, 1, 2, 3), (2, 3, 0, 1))
    def gather_own(phase, buffer, size):
        for k in range(MSG):
            for way in range(2):
                gather_copies(phase, buffer, size, mine, way, ORDER[way][k], 0).start()

    def gather_forward(phase, buffer, size):
        for k in range(MSG // 2):
            for way in range(2):
                m = ORDER[way][k]
                slot = slot_left if way == 0 else slot_right
                gather_copies(phase, buffer, size, slot, way, m, 0).wait_recv()
                gather_copies(phase, buffer, size, slot, way, m, 1).start()

    def gathered(phase, buffer, size):
        for k in range(MSG // 2, MSG):
            for way in range(2):
                slot = slot_left if way == 0 else slot_right
                gather_copies(phase, buffer, size, slot, way, ORDER[way][k], 0).wait_recv()
        for k in range(MSG // 2):
            for way in range(2):
                gather_copies(phase, buffer, size, slot_far, way, ORDER[way][k], 1).wait_recv()

    def land_whole(source):
        return parts.at[mine, source]

    def land_mixed(source):
        return mixed.at[source]

    for i in range(AHEAD):
        begin(jnp.int32(i))
    for load in loads[1:]:
        load.wait()
    for i in range(STEPS):
        if i + AHEAD < STEPS:
            begin(jnp.int32(i + AHEAD))
        add(jnp.int32(i))
        if i >= 1:
            update(jnp.int32(i - 1))
        if i == 4:
            exchange(0, land_whole)
    exchanged(0, land_whole)
    gather_own(0, parts, 32 // MSG)
    update(jnp.int32(STEPS - 1))
    exchange(1, land_mixed)
    gather_forward(0, parts, 32 // MSG)
    exchanged(1, land_mixed)

    lane = lax.broadcasted_iota(jnp.int32, (WIDE, LANE), 1)

    def merge(g, carry):
        for a in range(3):
            whole[mine, 3 * g + a] = jnp.where(
                lane < LANE - PIECE - PIECE * a, mixed[4 * g + a], mixed[4 * g + a + 1]
            )
        return carry

    lax.fori_loop(0, 8, merge, 0)
    gather_own(1, whole, MERGED // MSG)
    gathered(0, parts, 32 // MSG)

    def put_parts(g, carry):
        for b in range(NB):
            for a in range(4):
                lanes = pl.ds(pl.multiple_of((7 * g + 2 * a) * LANE, LANE), LANE)
                rollout[b, :, lanes] = parts[plan[b], 4 * g + a]
        return carry

    lax.fori_loop(0, 8, put_parts, 0)
    gather_forward(1, whole, MERGED // MSG)
    gathered(1, whole, MERGED // MSG)

    def put_whole(g, carry):
        for b in range(NB):
            for a in range(3):
                lanes = pl.ds(pl.multiple_of((7 * g + 2 * a + 1) * LANE, LANE), LANE)
                rollout[b, :, lanes] = whole[plan[b], 3 * g + a]
        return carry

    lax.fori_loop(0, 8, put_whole, 0)

    for i in range(STEPS):
        for copy in relays(jnp.int32(i)) + raws(jnp.int32(i)) + sums(jnp.int32(i)):
            copy.wait_send()
    for phase, landing in ((0, land_whole), (1, land_mixed)):
        everything = landing(pl.ds(0, SHARDS - 1))
        remote(everything, everything, x_send.at[phase], x_recv.at[phase], right).wait_send()
    for phase, buffer, size in ((0, parts, 32 // MSG), (1, whole, MERGED // MSG)):
        for k in range(MSG):
            for way in range(2):
                gather_copies(phase, buffer, size, mine, way, ORDER[way][k], 0).wait_send()
        for k in range(MSG // 2):
            for way in range(2):
                slot = slot_left if way == 0 else slot_right
                gather_copies(phase, buffer, size, slot, way, ORDER[way][k], 1).wait_send()


def write_kernel(*refs):
    sources, results, sems = refs[:4], refs[4:8], refs[8]
    copies = [pltpu.make_async_copy(s, r, sems.at[i]) for i, (s, r) in enumerate(zip(sources, results))]
    for copy in copies:
        copy.start()
    for copy in copies:
        copy.wait()


def body(grad_parts, master, moment, variance, plan, step):
    hbm = pl.BlockSpec(memory_space=pltpu.HBM)
    vmem = pl.BlockSpec(memory_space=pltpu.VMEM)
    smem = pl.BlockSpec(memory_space=pltpu.SMEM)
    state = jax.ShapeDtypeStruct((ROWS, COLS), F32)
    outs = [state, state, state, jax.ShapeDtypeStruct((NB, WIDE, SHARDS * ROWS), BF16)]
    dma = pltpu.SemaphoreType.DMA
    results = pl.pallas_call(
        main_kernel,
        out_shape=outs,
        in_specs=[smem, smem] + [hbm] * 4,
        out_specs=[vmem] * 4,
        scratch_shapes=[
            pltpu.VMEM((NB, ROWS, COLS), BF16),
            pltpu.VMEM((ROWS, COLS), F32),
            pltpu.VMEM((ROWS, COLS), F32),
            pltpu.VMEM((ROWS, COLS), F32),
            pltpu.VMEM((ROWS, COLS), BF16),
            pltpu.VMEM((ROWS, COLS), BF16),
            pltpu.VMEM((ROWS, COLS), BF16),
            pltpu.VMEM((ROWS, HALF), BF16),
            pltpu.VMEM((ROWS, HALF), BF16),
            pltpu.VMEM((ROWS, COLS), BF16),
            pltpu.VMEM((ROWS, COLS), BF16),
            pltpu.VMEM((2, COLS, LANE), BF16),
            pltpu.VMEM((NB, SHARDS, WIDE, LANE), BF16),
            pltpu.VMEM((NB, MERGED, WIDE, LANE), BF16),
            pltpu.VMEM((SHARDS, WIDE, LANE), BF16),
            dma((4,)),
            dma((STEPS, 2)),
            dma((STEPS, 2)),
            dma((STEPS, 2)),
            dma((STEPS, 2)),
            dma((STEPS, 2)),
            dma((STEPS, 2)),
            dma((2,)),
            dma((2,)),
            dma((2, 2, 2, MSG)),
            dma((2, 2, 2, MSG)),
        ],
        compiler_params=pltpu.CompilerParams(
            collective_id=0, has_side_effects=True, vmem_limit_bytes=26 << 20
        ),
        name="update_and_hand_off",
    )(plan, step, *[pltpu.with_memory_space_constraint(x[0], pltpu.HBM) for x in (grad_parts, master, moment, variance)])
    new_master, new_moment, new_variance, rollout = pl.pallas_call(
        write_kernel,
        out_shape=outs,
        in_specs=[vmem] * 4,
        out_specs=[hbm] * 4,
        scratch_shapes=[dma((4,))],
        compiler_params=pltpu.CompilerParams(vmem_limit_bytes=16 << 20),
        name="write_results",
    )(*results)
    return (new_master[None], new_moment[None], new_variance[None], rollout)


def solution(mesh):
    return jax.shard_map(
        body,
        mesh=mesh,
        in_specs=(
            P(("side", "group"), None, "shard", None),
            P(("side", "group"), "shard", None),
            P(("side", "group"), "shard", None),
            P(("side", "group"), "shard", None),
            P(),
            P(),
        ),
        out_specs=(
            P(("side", "group"), "shard", None),
            P(("side", "group"), "shard", None),
            P(("side", "group"), "shard", None),
            P(None, "shard", None),
        ),
        check_vma=False,
    )
```

time: 391 us -> 81.2 us (0.21)
  waiting for transfers between devices: 260 us -> 0 us
  Pallas kernels: 0 us -> 79.1 us
  blocking collectives: 60.1 us -> 0 us
  local copies, waits for them, and re-layouts: 38 us -> 1.3 us
  other arithmetic: 14.8 us -> 0 us
  between operations: 15.2 us -> 0.65 us
    psum x4 -> x0, waiting for transfers between devices: 186 us -> none  [from_root(): return lax.psum(jnp.where(mine, shard, jnp.zeros_like(shard)), axis)]
    pallas_call x0 -> x2, Pallas kernels: none -> 79.1 us  [the longest x1 75.4 us: body(): pl.pallas_call(main_kernel, out_shape=outs, in_specs=[smem, smem] + [hbm]...]
    reduce_scatter x1 -> x0, waiting for transfers between devices: 73.1 us -> none  [body(): lax.psum_scatter(ordered, ('side', 'group'), scatter_dimension=0, tiled=T...]
    all_to_all x1 -> x0, blocking collectives: 60.1 us -> none  [body(): lax.all_to_all(flipped, 'shard', split_axis=1, concat_axis=2, tiled=True)]
    all_to_all x3 -> x0, local copies, waits for them, and re-layouts: 13.7 us -> none  [body(): lax.all_to_all(flipped, 'shard', split_axis=1, concat_axis=2, tiled=True)]
    dynamic_update_slice x4 -> x0, local copies, waits for them, and re-layouts: 8.84 us -> none  [one_matrix(): return lax.dynamic_update_index_in_dim(result, got, index, 0)]
    select_n x6 -> x0, other arithmetic: 8.24 us -> none  [the longest x2 4.29 us: body(): ordered = jnp.take(grad_parts[0], matrix_of_slot, axis=0)]
    while x1 -> x0, local copies, waits for them, and re-layouts: 7.28 us -> none  [spread(): return lax.fori_loop(0, total, one_matrix, start)]
  transfers between devices with their start and end apart: 5 -> 0, of which waited for: 5 -> 0; matrix products, arithmetic and copies ran while one was open for 0% -> 0% of each run, Pallas kernels for 0% -> 0%
where the time goes in v1:
time: 81.2 us; the launch traced here: 81.1 us
  Pallas kernels  79.1 us (97%)
  local copies, waits for them, and re-layouts  1.3 us (2%)
    pallas_call x1, Pallas kernels, body(): pl.pallas_call(main_kernel, out_shape=outs, in_specs=[smem, smem] + [hbm]...  75.4 us
    pallas_call x1, Pallas kernels, body(): pl.pallas_call(write_kernel, out_shape=outs, in_specs=[vmem] * 4, out_spe...  3.68 us

profile of v1, /device:TPU:1, one launch (start us, length us, event | category | flops | bytes accessed | tf_op | source)
XLA Modules:
  0.0 81.1 jit_solution(11810184880704069651)
XLA Ops:
  0.6 0.0 copy-start
  0.6 0.6 copy-done
  1.3 0.0 copy-start.1
  1.3 0.7 copy-done.1
  1.9 75.4 %update_and_hand_off.1 = (f32[224,2048]{1,0:T(8,128)S(1)}, f32[224,2048]{1,0:T(8,128)S(1)}, f32[224,2048]{1,0:T(8,128)S(1)}, bf16[4,64,7168]{2,1,0:T(8,128)(2,1)S(1)}) custom-call(s32[4]{0:T(128)S(1)} %copy-done, s32[4]{0:T(128)S(1)} %copy-done.1, bf16[4,224,2048]{2,1,0:T(8,128)(2,1)} %bitcast.7, f32[224,2048]{1,0:T(8,128)} %bitcast.8, f32[224,2048]{1,0:T(8,128)} %bitcast.9, ...), custom_call_target="tpu_custom_call" | custom-call | tf_op jit(solution)/shard_map/update_and_hand_off/pallas_call | solution.py:339
  77.4 3.7 %write_results.1 = (f32[224,2048]{1,0:T(8,128)}, f32[224,2048]{1,0:T(8,128)}, f32[224,2048]{1,0:T(8,128)}, bf16[4,64,7168]{2,1,0:T(8,128)(2,1)}) custom-call(f32[224,2048]{1,0:T(8,128)S(1)} %get-tuple-element.12.refs_0_, f32[224,2048]{1,0:T(8,128)S(1)} %get-tuple-element.13.refs_1_, f32[224,2048]{1,0:T(8,128)S(1)} %get-tuple-element.14.refs_2_, ...), custom_call_target="tpu_custom_call" | custom-call | tf_op jit(solution)/shard_map/write_results/pallas_call | solution.py:377
Async XLA Ops:
  0.6 0.7 copy-start
  1.3 0.7 copy-start.1

commit v2 on v1

--- a/solution.py
+++ b/solution.py
@@ -18,13 +18,13 @@
 HALF = COLS // 2
 PIECE = 32
 STEPS = ROWS // PIECE
+EARLY = 2
 WIDE = 64
 LANE = 128
 SHARDS = 32
 NB = 4
 MERGED = 24
 MSG = 4
-AHEAD = 2
 MESH = pl.DeviceIdType.MESH
 BF16 = jnp.bfloat16
 F32 = jnp.float32
@@ -41,12 +41,12 @@
 
 
 def main_kernel(
-    plan, step, grad_hbm, master_hbm, moment_hbm, variance_hbm,
+    plan_hbm, step_hbm, grad_hbm, master_hbm, moment_hbm, variance_hbm,
     new_master, new_moment, new_variance, rollout,
-    grad, master, moment, variance,
+    plan, step, grad, early, master, moment, variance,
     to_opposite, to_right, to_left, relay_left, relay_right, from_left, from_right,
     turned, parts, whole, mixed,
-    load_sem, s_sem, relay_sem, raw_sem, sum_sem, s_raw_sem, s_sum_sem,
+    load_sem, plane_sem, s_sem, relay_sem, raw_sem, sum_sem, s_raw_sem, s_sum_sem,
     x_send, x_recv, g_send, g_recv,
 ):
     side, group, shard = lax.axis_index("side"), lax.axis_index("group"), lax.axis_index("shard")
@@ -63,25 +63,30 @@
     right, left = place(z_right, shard), place(z_left, shard)
     mine, slot_right, slot_left, slot_far = slot_of(z), slot_of(z_right), slot_of(z_left), slot_of(z_far)
 
+    fetches = [
+        pltpu.make_async_copy(plan_hbm, plan, load_sem.at[4]),
+        pltpu.make_async_copy(step_hbm, step, load_sem.at[5]),
+        pltpu.make_async_copy(
+            grad_hbm.at[:, pl.ds(pl.multiple_of(turn * PIECE, PIECE), EARLY * PIECE), :], early, load_sem.at[6]
+        ),
+    ]
     loads = [
         pltpu.make_async_copy(grad_hbm, grad, load_sem.at[0]),
         pltpu.make_async_copy(master_hbm, master, load_sem.at[1]),
         pltpu.make_async_copy(moment_hbm, moment, load_sem.at[2]),
         pltpu.make_async_copy(variance_hbm, variance, load_sem.at[3]),
     ]
-    for load in loads:
+    for load in fetches + loads:
         load.start()
 
+    row, column = shard // 8, lax.rem(shard, 8)
+    across = [place(z, lax.rem(row + k, 4) * 8 + column) for k in range(1, 4)]
     barrier = pltpu.get_barrier_semaphore()
-    pl.semaphore_signal(barrier, inc=1, device_id=right, device_id_type=MESH)
-    pl.semaphore_signal(barrier, inc=1, device_id=left, device_id_type=MESH)
-
-    def greet(offset, carry):
-        other = lax.rem(shard + offset, SHARDS)
-        pl.semaphore_signal(barrier, inc=1, device_id=place(z, other), device_id_type=MESH)
-        return carry
-
-    lax.fori_loop(1, SHARDS, greet, 0)
+    for other in [right, left] + across + [place(z, row * 8 + lax.rem(column + k, 8)) for k in range(1, 8)]:
+        pl.semaphore_signal(barrier, inc=1, device_id=other, device_id_type=MESH)
+
+    for load in fetches:
+        load.wait()
 
     def matrix_of(slot):
         found = jnp.int32(0)
@@ -94,9 +99,6 @@
     one = jnp.ones((1, LANE), F32)
     first_scale = one / (one * (1.0 - power(BETA_ONE, count)))
     second_scale = one / (one * (1.0 - power(BETA_TWO, count)))
-
-    loads[0].wait()
-    pl.semaphore_wait(barrier, SHARDS + 1)
 
     def rows_at(position):
         segment = lax.rem(turn + position, 8)
@@ -134,12 +136,20 @@
             remote(to_left.at[rows, high], from_right.at[rows, high], s_sum_sem.at[i, 1], sum_sem.at[i, 1], left),
         )
 
-    def begin(i):
-        rows = rows_of(i)
-        to_opposite[rows, :] = grad[b_far, rows, :]
-        to_right[rows, high] = grad[b_right, rows, high]
-        to_left[rows, low] = grad[b_left, rows, low]
-        for copy in relays(i) + raws(i):
+    def staged(i):
+        return (early, pl.ds(i * PIECE, PIECE)) if i < EARLY else (grad, rows_of(jnp.int32(i)))
+
+    def stage_relays(i):
+        source, at = staged(i)
+        to_opposite[rows_of(jnp.int32(i)), :] = source[b_far, at, :]
+
+    def stage_raws(i):
+        source, at = staged(i)
+        to_right[rows_of(jnp.int32(i)), high] = source[b_right, at, high]
+        to_left[rows_of(jnp.int32(i)), low] = source[b_left, at, low]
+
+    def start(copies):
+        for copy in copies:
             copy.start()
 
     def add(i):
@@ -252,20 +262,33 @@
     def land_mixed(source):
         return mixed.at[source]
 
-    for i in range(AHEAD):
-        begin(jnp.int32(i))
-    for load in loads[1:]:
-        load.wait()
+    stage_relays(0)
+    stage_raws(0)
+    pl.semaphore_wait(barrier, 12)
+    start(relays(jnp.int32(0)) + raws(jnp.int32(0)))
+    for other in across:
+        pl.semaphore_signal(plane_sem, inc=1, device_id=other, device_id_type=MESH)
     for i in range(STEPS):
-        if i + AHEAD < STEPS:
-            begin(jnp.int32(i + AHEAD))
+        if i + 1 < STEPS:
+            stage_relays(i + 1)
+            start(relays(jnp.int32(i + 1)))
+        if i == 0:
+            loads[0].wait()
         add(jnp.int32(i))
-        if i >= 1:
+        if i + 1 < STEPS:
+            stage_raws(i + 1)
+            start(raws(jnp.int32(i + 1)))
+        if i == 1:
+            for load in loads[1:]:
+                load.wait()
+            pl.semaphore_wait(plane_sem, 3)
+        if 1 <= i < STEPS - 1:
             update(jnp.int32(i - 1))
         if i == 4:
             exchange(0, land_whole)
     exchanged(0, land_whole)
     gather_own(0, parts, 32 // MSG)
+    update(jnp.int32(STEPS - 2))
     update(jnp.int32(STEPS - 1))
     exchange(1, land_mixed)
     gather_forward(0, parts, 32 // MSG)
@@ -282,6 +305,12 @@
 
     lax.fori_loop(0, 8, merge, 0)
     gather_own(1, whole, MERGED // MSG)
+    for i in range(STEPS):
+        for copy in relays(jnp.int32(i)) + raws(jnp.int32(i)) + sums(jnp.int32(i)):
+            copy.wait_send()
+    for phase, landing in ((0, land_whole), (1, land_mixed)):
+        everything = landing(pl.ds(0, SHARDS - 1))
+        remote(everything, everything, x_send.at[phase], x_recv.at[phase], right).wait_send()
     gathered(0, parts, 32 // MSG)
 
     def put_parts(g, carry):
@@ -304,12 +333,6 @@
 
     lax.fori_loop(0, 8, put_whole, 0)
 
-    for i in range(STEPS):
-        for copy in relays(jnp.int32(i)) + raws(jnp.int32(i)) + sums(jnp.int32(i)):
-            copy.wait_send()
-    for phase, landing in ((0, land_whole), (1, land_mixed)):
-        everything = landing(pl.ds(0, SHARDS - 1))
-        remote(everything, everything, x_send.at[phase], x_recv.at[phase], right).wait_send()
     for phase, buffer, size in ((0, parts, 32 // MSG), (1, whole, MERGED // MSG)):
         for k in range(MSG):
             for way in range(2):
@@ -332,17 +355,19 @@
 def body(grad_parts, master, moment, variance, plan, step):
     hbm = pl.BlockSpec(memory_space=pltpu.HBM)
     vmem = pl.BlockSpec(memory_space=pltpu.VMEM)
-    smem = pl.BlockSpec(memory_space=pltpu.SMEM)
     state = jax.ShapeDtypeStruct((ROWS, COLS), F32)
     outs = [state, state, state, jax.ShapeDtypeStruct((NB, WIDE, SHARDS * ROWS), BF16)]
     dma = pltpu.SemaphoreType.DMA
     results = pl.pallas_call(
         main_kernel,
         out_shape=outs,
-        in_specs=[smem, smem] + [hbm] * 4,
+        in_specs=[hbm] * 6,
         out_specs=[vmem] * 4,
         scratch_shapes=[
+            pltpu.SMEM((NB,), jnp.int32),
+            pltpu.SMEM((NB,), jnp.int32),
             pltpu.VMEM((NB, ROWS, COLS), BF16),
+            pltpu.VMEM((NB, EARLY * PIECE, COLS), BF16),
             pltpu.VMEM((ROWS, COLS), F32),
             pltpu.VMEM((ROWS, COLS), F32),
             pltpu.VMEM((ROWS, COLS), F32),
@@ -357,7 +382,8 @@
             pltpu.VMEM((NB, SHARDS, WIDE, LANE), BF16),
             pltpu.VMEM((NB, MERGED, WIDE, LANE), BF16),
             pltpu.VMEM((SHARDS, WIDE, LANE), BF16),
-            dma((4,)),
+            dma((7,)),
+            pltpu.SemaphoreType.REGULAR,
             dma((STEPS, 2)),
             dma((STEPS, 2)),
             dma((STEPS, 2)),
@@ -370,10 +396,10 @@
             dma((2, 2, 2, MSG)),
         ],
         compiler_params=pltpu.CompilerParams(
-            collective_id=0, has_side_effects=True, vmem_limit_bytes=26 << 20
+            collective_id=0, has_side_effects=True, vmem_limit_bytes=28 << 20
         ),
         name="update_and_hand_off",
-    )(plan, step, *[pltpu.with_memory_space_constraint(x[0], pltpu.HBM) for x in (grad_parts, master, moment, variance)])
+    )(*[pltpu.with_memory_space_constraint(x, pltpu.HBM) for x in (plan, step, grad_parts[0], master[0], moment[0], variance[0])])
     new_master, new_moment, new_variance, rollout = pl.pallas_call(
         write_kernel,
         out_shape=outs,

time: 81.2 us -> 74.8 us (0.921)
  Pallas kernels: 79.1 us -> 74 us
  local copies, waits for them, and re-layouts: 1.3 us -> 0 us
    pallas_call x1, Pallas kernels: 75.4 us -> 70.3 us  [body(): pl.pallas_call(main_kernel, out_shape=outs, in_specs=[hbm] * 6, out_specs...]
    unnamed x4 -> x0, local copies, waits for them, and re-layouts: 1.3 us -> none
where the time goes in v2:
time: 74.8 us; the launch traced here: 74.6 us
  Pallas kernels  74 us (99%)
    pallas_call x1, Pallas kernels, body(): pl.pallas_call(main_kernel, out_shape=outs, in_specs=[hbm] * 6, out_specs...  70.3 us
    pallas_call x1, Pallas kernels, body(): pl.pallas_call(write_kernel, out_shape=outs, in_specs=[vmem] * 4, out_spe...  3.68 us

profile of v2, /device:TPU:1, one launch (start us, length us, event | category | flops | bytes accessed | tf_op | source)
XLA Modules:
  0.0 74.6 jit_solution(3331884869574988849)
XLA Ops:
  0.6 70.3 %update_and_hand_off.1 = (f32[224,2048]{1,0:T(8,128)S(1)}, f32[224,2048]{1,0:T(8,128)S(1)}, f32[224,2048]{1,0:T(8,128)S(1)}, bf16[4,64,7168]{2,1,0:T(8,128)(2,1)S(1)}) custom-call(s32[4]{0:T(128)} %plan_hbm.1, s32[4]{0:T(128)} %step_hbm.1, bf16[4,224,2048]{2,1,0:T(8,128)(2,1)} %bitcast.7, f32[224,2048]{1,0:T(8,128)} %bitcast.8, f32[224,2048]{1,0:T(8,128)} %bitcast.9, ...), custom_call_target="tpu_custom_call" | custom-call | tf_op jit(solution)/shard_map/update_and_hand_off/pallas_call | solution.py:361
  71.0 3.7 %write_results.1 = (f32[224,2048]{1,0:T(8,128)}, f32[224,2048]{1,0:T(8,128)}, f32[224,2048]{1,0:T(8,128)}, bf16[4,64,7168]{2,1,0:T(8,128)(2,1)}) custom-call(f32[224,2048]{1,0:T(8,128)S(1)} %get-tuple-element.12.refs_0_, f32[224,2048]{1,0:T(8,128)S(1)} %get-tuple-element.13.refs_1_, f32[224,2048]{1,0:T(8,128)S(1)} %get-tuple-element.14.refs_2_, ...), custom_call_target="tpu_custom_call" | custom-call | tf_op jit(solution)/shard_map/write_results/pallas_call | solution.py:403

commit v3 on v2

--- a/solution.py
+++ b/solution.py
@@ -18,7 +18,8 @@
 HALF = COLS // 2
 PIECE = 32
 STEPS = ROWS // PIECE
-EARLY = 2
+GROUP = 512
+FULL = 4 * PIECE
 WIDE = 64
 LANE = 128
 SHARDS = 32
@@ -44,7 +45,7 @@
     plan_hbm, step_hbm, grad_hbm, master_hbm, moment_hbm, variance_hbm,
     new_master, new_moment, new_variance, rollout,
     plan, step, grad, early, master, moment, variance,
-    to_opposite, to_right, to_left, relay_left, relay_right, from_left, from_right,
+    to_opposite, to_right, to_left, relay, from_left, from_right,
     turned, parts, whole, mixed,
     load_sem, plane_sem, s_sem, relay_sem, raw_sem, sum_sem, s_raw_sem, s_sum_sem,
     x_send, x_recv, g_send, g_recv,
@@ -63,11 +64,16 @@
     right, left = place(z_right, shard), place(z_left, shard)
     mine, slot_right, slot_left, slot_far = slot_of(z), slot_of(z_right), slot_of(z_left), slot_of(z_far)
 
+    row, column = shard // 8, lax.rem(shard, 8)
+
+    def group_of(i):
+        return pl.ds(pl.multiple_of(lax.rem(row + i, 4) * GROUP, GROUP), GROUP)
+
     fetches = [
         pltpu.make_async_copy(plan_hbm, plan, load_sem.at[4]),
         pltpu.make_async_copy(step_hbm, step, load_sem.at[5]),
         pltpu.make_async_copy(
-            grad_hbm.at[:, pl.ds(pl.multiple_of(turn * PIECE, PIECE), EARLY * PIECE), :], early, load_sem.at[6]
+            grad_hbm.at[:, pl.ds(pl.multiple_of(turn * PIECE, PIECE), FULL), group_of(0)], early, load_sem.at[6]
         ),
     ]
     loads = [
@@ -79,11 +85,75 @@
     for load in fetches + loads:
         load.start()
 
-    row, column = shard // 8, lax.rem(shard, 8)
+    along = [place(z, row * 8 + lax.rem(column + k, 8)) for k in range(1, 8)]
     across = [place(z, lax.rem(row + k, 4) * 8 + column) for k in range(1, 4)]
     barrier = pltpu.get_barrier_semaphore()
-    for other in [right, left] + across + [place(z, row * 8 + lax.rem(column + k, 8)) for k in range(1, 8)]:
-        pl.semaphore_signal(barrier, inc=1, device_id=other, device_id_type=MESH)
+
+    def signal(semaphore, others):
+        for other in others:
+            pl.semaphore_signal(semaphore, inc=1, device_id=other, device_id_type=MESH)
+
+    signal(barrier, [right, left])
+
+    @pl.when(z == 0)
+    def _():
+        signal(barrier, along)
+
+    @pl.when(z == 1)
+    def _():
+        signal(barrier, across)
+
+    def tell(stage):
+        if stage == 0:
+
+            @pl.when(z == 1)
+            def _():
+                signal(plane_sem.at[0], [left])
+
+        if stage == 1:
+
+            @pl.when(z == 0)
+            def _():
+                pl.semaphore_wait(plane_sem.at[0], 1)
+                signal(plane_sem.at[1], along)
+
+        if stage == 2:
+
+            @pl.when(z == 0)
+            def _():
+                pl.semaphore_wait(plane_sem.at[1], 7)
+                signal(plane_sem.at[2], [right])
+
+        if stage == 3:
+
+            @pl.when(z == 1)
+            def _():
+                pl.semaphore_wait(plane_sem.at[2], 1)
+                signal(plane_sem.at[3], across)
+
+        if stage == 4:
+
+            @pl.when(z == 1)
+            def _():
+                pl.semaphore_wait(plane_sem.at[3], 3)
+                signal(plane_sem.at[4], [left, right])
+
+        if stage == 5:
+
+            @pl.when(z == 0)
+            def _():
+                pl.semaphore_wait(plane_sem.at[4], 1)
+
+            @pl.when(z == 2)
+            def _():
+                pl.semaphore_wait(plane_sem.at[4], 1)
+                signal(plane_sem.at[4], [right])
+
+        if stage == 6:
+
+            @pl.when(z == 3)
+            def _():
+                pl.semaphore_wait(plane_sem.at[4], 1)
 
     for load in fetches:
         load.wait()
@@ -104,11 +174,16 @@
         segment = lax.rem(turn + position, 8)
         return pl.multiple_of(jnp.minimum(segment, STEPS - 1) * PIECE, PIECE)
 
-    def rows_of(index):
-        position = index + jnp.where(index >= STEPS - turn, 1, 0)
-        return pl.ds(rows_at(position), PIECE)
-
-    low, high = pl.ds(0, HALF), pl.ds(HALF, HALF)
+    def rows_of(i):
+        if i < 4:
+            return pl.ds(pl.multiple_of(turn * PIECE, PIECE), FULL)
+        return pl.ds(rows_at(i + jnp.where(i >= STEPS - turn, 1, 0)), PIECE)
+
+    def half(i, k):
+        if i < 4:
+            first = lax.rem(row + i, 4) * GROUP + k * (GROUP // 2)
+            return rows_of(i), pl.ds(pl.multiple_of(first, GROUP // 2), GROUP // 2)
+        return rows_of(i), pl.ds(k * HALF, HALF)
 
     def remote(src, dst, send, recv, where):
         return pltpu.make_async_remote_copy(
@@ -116,62 +191,65 @@
         )
 
     def relays(i):
-        rows = rows_of(i)
+        low, high = half(i, 0), half(i, 1)
         return (
-            remote(to_opposite.at[rows, low], relay_left.at[rows, :], s_sem.at[i, 0], relay_sem.at[i, 0], right),
-            remote(to_opposite.at[rows, high], relay_right.at[rows, :], s_sem.at[i, 1], relay_sem.at[i, 1], left),
+            remote(to_opposite.at[low], relay.at[low], s_sem.at[i, 0], relay_sem.at[i, 0], right),
+            remote(to_opposite.at[high], relay.at[high], s_sem.at[i, 1], relay_sem.at[i, 1], left),
         )
 
     def raws(i):
-        rows = rows_of(i)
+        low, high = half(i, 0), half(i, 1)
         return (
-            remote(to_right.at[rows, high], from_left.at[rows, high], s_raw_sem.at[i, 0], raw_sem.at[i, 0], right),
-            remote(to_left.at[rows, low], from_right.at[rows, low], s_raw_sem.at[i, 1], raw_sem.at[i, 1], left),
+            remote(to_right.at[high], from_left.at[high], s_raw_sem.at[i, 0], raw_sem.at[i, 0], right),
+            remote(to_left.at[low], from_right.at[low], s_raw_sem.at[i, 1], raw_sem.at[i, 1], left),
         )
 
     def sums(i):
-        rows = rows_of(i)
+        low, high = half(i, 0), half(i, 1)
         return (
-            remote(to_right.at[rows, low], from_left.at[rows, low], s_sum_sem.at[i, 0], sum_sem.at[i, 0], right),
-            remote(to_left.at[rows, high], from_right.at[rows, high], s_sum_sem.at[i, 1], sum_sem.at[i, 1], left),
+            remote(to_right.at[low], from_left.at[low], s_sum_sem.at[i, 0], sum_sem.at[i, 0], right),
+            remote(to_left.at[high], from_right.at[high], s_sum_sem.at[i, 1], sum_sem.at[i, 1], left),
         )
 
-    def staged(i):
-        return (early, pl.ds(i * PIECE, PIECE)) if i < EARLY else (grad, rows_of(jnp.int32(i)))
+    def part_of(b, i, k):
+        if i == 0:
+            return early[b, :, pl.ds(k * (GROUP // 2), GROUP // 2)]
+        rows, lanes = half(i, k)
+        return grad[b, rows, lanes]
 
     def stage_relays(i):
-        source, at = staged(i)
-        to_opposite[rows_of(jnp.int32(i)), :] = source[b_far, at, :]
+        for k in range(2):
+            to_opposite[half(i, k)] = part_of(b_far, i, k)
 
     def stage_raws(i):
-        source, at = staged(i)
-        to_right[rows_of(jnp.int32(i)), high] = source[b_right, at, high]
-        to_left[rows_of(jnp.int32(i)), low] = source[b_left, at, low]
+        to_right[half(i, 1)] = part_of(b_right, i, 1)
+        to_left[half(i, 0)] = part_of(b_left, i, 0)
 
     def start(copies):
         for copy in copies:
             copy.start()
 
     def add(i):
-        rows = rows_of(i)
+        low, high = half(i, 0), half(i, 1)
         first, second = relays(i)
         to_r, to_l = sums(i)
         first.wait_recv()
-        own = grad[b_right, rows, low].astype(F32)
-        to_right[rows, low] = (relay_left[rows, :].astype(F32) + own).astype(BF16)
+        to_right[low] = (relay[low].astype(F32) + part_of(b_right, i, 0).astype(F32)).astype(BF16)
         to_r.start()
         second.wait_recv()
-        own = grad[b_left, rows, high].astype(F32)
-        to_left[rows, high] = (relay_right[rows, :].astype(F32) + own).astype(BF16)
+        to_left[high] = (relay[high].astype(F32) + part_of(b_left, i, 1).astype(F32)).astype(BF16)
         to_l.start()
 
     def update(i):
-        rows = rows_of(i)
         for copy in raws(i) + sums(i):
             copy.wait_recv()
 
         def tile(j, carry):
-            lanes = pl.ds(pl.multiple_of(j * LANE, LANE), LANE)
+            if i < 4:
+                rows = pl.ds(pl.multiple_of((turn + j // 4) * PIECE, PIECE), PIECE)
+                lanes = pl.ds(pl.multiple_of(lax.rem(row + i, 4) * GROUP + lax.rem(j, 4) * LANE, LANE), LANE)
+            else:
+                rows, lanes = rows_of(i), pl.ds(pl.multiple_of(j * LANE, LANE), LANE)
             total = (
                 grad[b_mine, rows, lanes].astype(F32)
                 + from_left[rows, lanes].astype(F32)
@@ -188,15 +266,16 @@
 
         lax.fori_loop(0, COLS // LANE, tile, 0)
 
-    def exchange(phase, landing):
-        my_chip, core = shard // 2, lax.rem(shard, 2)
+    def exchange(phase, landing, i):
+        first = lax.rem(row + i, 4) * 4
+        my_chip = lax.rem(shard, 8) // 2
 
         def turn_chip(chip):
             lanes = pl.ds(pl.multiple_of(chip * LANE, LANE), LANE)
             block = jnp.concatenate(
                 [new_master[pl.ds(rows_at(4 * phase + q), PIECE), lanes] for q in range(4)], axis=0
             )
-            turned[phase, pl.ds(pl.multiple_of(chip * LANE, LANE), LANE), :] = block.T.astype(BF16)
+            turned[phase, lanes, :] = block.T.astype(BF16)
 
         def source(other):
             return turned.at[phase, pl.ds(pl.multiple_of(other * WIDE, WIDE), WIDE), :]
@@ -204,25 +283,21 @@
         def send(other):
             remote(source(other), landing(shard), x_send.at[phase], x_recv.at[phase], place(z, other)).start()
 
-        turn_chip(my_chip)
-
-        def one(k, carry):
-            turn_chip(lax.rem(my_chip + k, SHARDS // 2))
-
-            @pl.when(k > 1)
-            def _():
-                before = lax.rem(my_chip + k - 1, SHARDS // 2)
-                send(before * 2)
-                send(before * 2 + 1)
-
-            return carry
-
-        lax.fori_loop(1, SHARDS // 2, one, 0)
-        last = lax.rem(my_chip + SHARDS // 2 - 1, SHARDS // 2)
-        send(last * 2)
-        send(last * 2 + 1)
-        send(my_chip * 2 + 1 - core)
-        landing(shard)[...] = turned[phase, pl.ds(pl.multiple_of(shard * WIDE, WIDE), WIDE), :]
+        def send_chip(k):
+            if i == 0 and k == 0:
+                send(shard + 1 - 2 * lax.rem(shard, 2))
+            else:
+                chip = first + lax.rem(my_chip + k, 4)
+                send(chip * 2)
+                send(chip * 2 + 1)
+
+        for k in range(4):
+            turn_chip(first + lax.rem(my_chip + k, 4))
+            if k > 0:
+                send_chip(k - 1)
+        send_chip(3)
+        if i == 0:
+            landing(shard)[...] = turned[phase, pl.ds(pl.multiple_of(shard * WIDE, WIDE), WIDE), :]
 
     def exchanged(phase, landing):
         everything = landing(pl.ds(0, SHARDS - 1))
@@ -264,33 +339,45 @@
 
     stage_relays(0)
     stage_raws(0)
-    pl.semaphore_wait(barrier, 12)
-    start(relays(jnp.int32(0)) + raws(jnp.int32(0)))
-    for other in across:
-        pl.semaphore_signal(plane_sem, inc=1, device_id=other, device_id_type=MESH)
+    pl.semaphore_wait(barrier, 2 + jnp.where(z == 0, 7, 0) + jnp.where(z == 1, 3, 0))
+    start(relays(0) + raws(0))
+    tell(0)
     for i in range(STEPS):
+        if i == 0:
+            loads[0].wait()
         if i + 1 < STEPS:
             stage_relays(i + 1)
-            start(relays(jnp.int32(i + 1)))
-        if i == 0:
-            loads[0].wait()
-        add(jnp.int32(i))
+            start(relays(i + 1))
+        if i == 1:
+            tell(2)
+        if i == 2:
+            tell(5)
+        add(i)
         if i + 1 < STEPS:
             stage_raws(i + 1)
-            start(raws(jnp.int32(i + 1)))
+            start(raws(i + 1))
+        if i == 0:
+            tell(1)
+        if i == 1:
+            tell(3)
+        if i == 2:
+            tell(6)
         if i == 1:
             for load in loads[1:]:
                 load.wait()
-            pl.semaphore_wait(plane_sem, 3)
         if 1 <= i < STEPS - 1:
-            update(jnp.int32(i - 1))
-        if i == 4:
-            exchange(0, land_whole)
+            update(i - 1)
+        if i == 1:
+            tell(4)
+        if 2 <= i <= 4:
+            for k in range(0 if i == 2 else i - 1, i):
+                exchange(0, land_whole, k)
     exchanged(0, land_whole)
     gather_own(0, parts, 32 // MSG)
-    update(jnp.int32(STEPS - 2))
-    update(jnp.int32(STEPS - 1))
-    exchange(1, land_mixed)
+    update(STEPS - 2)
+    update(STEPS - 1)
+    for i in range(4):
+        exchange(1, land_mixed, i)
     gather_forward(0, parts, 32 // MSG)
     exchanged(1, land_mixed)
 
@@ -306,7 +393,7 @@
     lax.fori_loop(0, 8, merge, 0)
     gather_own(1, whole, MERGED // MSG)
     for i in range(STEPS):
-        for copy in relays(jnp.int32(i)) + raws(jnp.int32(i)) + sums(jnp.int32(i)):
+        for copy in relays(i) + raws(i) + sums(i):
             copy.wait_send()
     for phase, landing in ((0, land_whole), (1, land_mixed)):
         everything = landing(pl.ds(0, SHARDS - 1))
@@ -367,15 +454,14 @@
             pltpu.SMEM((NB,), jnp.int32),
             pltpu.SMEM((NB,), jnp.int32),
             pltpu.VMEM((NB, ROWS, COLS), BF16),
-            pltpu.VMEM((NB, EARLY * PIECE, COLS), BF16),
+            pltpu.VMEM((NB, FULL, GROUP), BF16),
             pltpu.VMEM((ROWS, COLS), F32),
             pltpu.VMEM((ROWS, COLS), F32),
             pltpu.VMEM((ROWS, COLS), F32),
             pltpu.VMEM((ROWS, COLS), BF16),
             pltpu.VMEM((ROWS, COLS), BF16),
             pltpu.VMEM((ROWS, COLS), BF16),
-            pltpu.VMEM((ROWS, HALF), BF16),
-            pltpu.VMEM((ROWS, HALF), BF16),
+            pltpu.VMEM((ROWS, COLS), BF16),
             pltpu.VMEM((ROWS, COLS), BF16),
             pltpu.VMEM((ROWS, COLS), BF16),
             pltpu.VMEM((2, COLS, LANE), BF16),
@@ -383,7 +469,7 @@
             pltpu.VMEM((NB, MERGED, WIDE, LANE), BF16),
             pltpu.VMEM((SHARDS, WIDE, LANE), BF16),
             dma((7,)),
-            pltpu.SemaphoreType.REGULAR,
+            pltpu.SemaphoreType.REGULAR((5,)),
             dma((STEPS, 2)),
             dma((STEPS, 2)),
             dma((STEPS, 2)),

time: 74.8 us -> 72.1 us (0.964)
  Pallas kernels: 74 us -> 71.3 us
    pallas_call x1, Pallas kernels: 70.3 us -> 67.6 us  [body(): pl.pallas_call(main_kernel, out_shape=outs, in_specs=[hbm] * 6, out_specs...]
where the time goes in v3:
time: 72.1 us; the launch traced here: 71.9 us
  Pallas kernels  71.3 us (99%)
    pallas_call x1, Pallas kernels, body(): pl.pallas_call(main_kernel, out_shape=outs, in_specs=[hbm] * 6, out_specs...  67.6 us
    pallas_call x1, Pallas kernels, body(): pl.pallas_call(write_kernel, out_shape=outs, in_specs=[vmem] * 4, out_spe...  3.68 us

profile of v3, /device:TPU:1, one launch (start us, length us, event | category | flops | bytes accessed | tf_op | source)
XLA Modules:
  0.0 71.9 jit_solution(7168470775747589275)
XLA Ops:
  0.6 67.6 %update_and_hand_off.1 = (f32[224,2048]{1,0:T(8,128)S(1)}, f32[224,2048]{1,0:T(8,128)S(1)}, f32[224,2048]{1,0:T(8,128)S(1)}, bf16[4,64,7168]{2,1,0:T(8,128)(2,1)S(1)}) custom-call(s32[4]{0:T(128)} %plan_hbm.1, s32[4]{0:T(128)} %step_hbm.1, bf16[4,224,2048]{2,1,0:T(8,128)(2,1)} %bitcast.7, f32[224,2048]{1,0:T(8,128)} %bitcast.8, f32[224,2048]{1,0:T(8,128)} %bitcast.9, ...), custom_call_target="tpu_custom_call" | custom-call | tf_op jit(solution)/shard_map/update_and_hand_off/pallas_call | solution.py:448
  68.3 3.7 %write_results.1 = (f32[224,2048]{1,0:T(8,128)}, f32[224,2048]{1,0:T(8,128)}, f32[224,2048]{1,0:T(8,128)}, bf16[4,64,7168]{2,1,0:T(8,128)(2,1)}) custom-call(f32[224,2048]{1,0:T(8,128)S(1)} %get-tuple-element.12.refs_0_, f32[224,2048]{1,0:T(8,128)S(1)} %get-tuple-element.13.refs_1_, f32[224,2048]{1,0:T(8,128)S(1)} %get-tuple-element.14.refs_2_, ...), custom_call_target="tpu_custom_call" | custom-call | tf_op jit(solution)/shard_map/write_results/pallas_call | solution.py:489

commit v4 on v3

--- a/solution.py
+++ b/solution.py
@@ -43,10 +43,10 @@
 
 def main_kernel(
     plan_hbm, step_hbm, grad_hbm, master_hbm, moment_hbm, variance_hbm,
-    new_master, new_moment, new_variance, rollout,
+    new_master, new_moment, new_variance, parts, whole,
     plan, step, grad, early, master, moment, variance,
     to_opposite, to_right, to_left, relay, from_left, from_right,
-    turned, parts, whole, mixed,
+    turned, mixed,
     load_sem, plane_sem, s_sem, relay_sem, raw_sem, sum_sem, s_raw_sem, s_sum_sem,
     x_send, x_recv, g_send, g_recv,
 ):
@@ -82,7 +82,7 @@
         pltpu.make_async_copy(moment_hbm, moment, load_sem.at[2]),
         pltpu.make_async_copy(variance_hbm, variance, load_sem.at[3]),
     ]
-    for load in fetches + loads:
+    for load in fetches:
         load.start()
 
     along = [place(z, row * 8 + lax.rem(column + k, 8)) for k in range(1, 8)]
@@ -157,6 +157,8 @@
 
     for load in fetches:
         load.wait()
+    for load in loads:
+        load.start()
 
     def matrix_of(slot):
         found = jnp.int32(0)
@@ -165,10 +167,6 @@
         return found
 
     b_mine, b_right, b_left, b_far = matrix_of(mine), matrix_of(slot_right), matrix_of(slot_left), matrix_of(slot_far)
-    count = step[b_mine]
-    one = jnp.ones((1, LANE), F32)
-    first_scale = one / (one * (1.0 - power(BETA_ONE, count)))
-    second_scale = one / (one * (1.0 - power(BETA_TWO, count)))
 
     def rows_at(position):
         segment = lax.rem(turn + position, 8)
@@ -338,10 +336,15 @@
         return mixed.at[source]
 
     stage_relays(0)
+    pl.semaphore_wait(barrier, 2 + jnp.where(z == 0, 7, 0) + jnp.where(z == 1, 3, 0))
+    start(relays(0))
     stage_raws(0)
-    pl.semaphore_wait(barrier, 2 + jnp.where(z == 0, 7, 0) + jnp.where(z == 1, 3, 0))
-    start(relays(0) + raws(0))
+    start(raws(0))
     tell(0)
+    count = step[b_mine]
+    one = jnp.ones((1, LANE), F32)
+    first_scale = one / (one * (1.0 - power(BETA_ONE, count)))
+    second_scale = one / (one * (1.0 - power(BETA_TWO, count)))
     for i in range(STEPS):
         if i == 0:
             loads[0].wait()
@@ -400,25 +403,8 @@
         remote(everything, everything, x_send.at[phase], x_recv.at[phase], right).wait_send()
     gathered(0, parts, 32 // MSG)
 
-    def put_parts(g, carry):
-        for b in range(NB):
-            for a in range(4):
-                lanes = pl.ds(pl.multiple_of((7 * g + 2 * a) * LANE, LANE), LANE)
-                rollout[b, :, lanes] = parts[plan[b], 4 * g + a]
-        return carry
-
-    lax.fori_loop(0, 8, put_parts, 0)
     gather_forward(1, whole, MERGED // MSG)
     gathered(1, whole, MERGED // MSG)
-
-    def put_whole(g, carry):
-        for b in range(NB):
-            for a in range(3):
-                lanes = pl.ds(pl.multiple_of((7 * g + 2 * a + 1) * LANE, LANE), LANE)
-                rollout[b, :, lanes] = whole[plan[b], 3 * g + a]
-        return carry
-
-    lax.fori_loop(0, 8, put_whole, 0)
 
     for phase, buffer, size in ((0, parts, 32 // MSG), (1, whole, MERGED // MSG)):
         for k in range(MSG):
@@ -430,13 +416,40 @@
                 gather_copies(phase, buffer, size, slot, way, ORDER[way][k], 1).wait_send()
 
 
-def write_kernel(*refs):
-    sources, results, sems = refs[:4], refs[4:8], refs[8]
-    copies = [pltpu.make_async_copy(s, r, sems.at[i]) for i, (s, r) in enumerate(zip(sources, results))]
-    for copy in copies:
+def write_kernel(
+    plan_hbm, master_in, moment_in, variance_in, parts, whole,
+    master, moment, variance, rollout, plan, plan_sem, sems,
+):
+    fetch = pltpu.make_async_copy(plan_hbm, plan, plan_sem)
+    fetch.start()
+    states = [
+        pltpu.make_async_copy(source, result, sems.at[i])
+        for i, (source, result) in enumerate(((master_in, master), (moment_in, moment), (variance_in, variance)))
+    ]
+    for copy in states:
         copy.start()
-    for copy in copies:
+    fetch.wait()
+
+    def start(source, b, block):
+        lanes = pl.ds(pl.multiple_of(block * LANE, LANE), LANE)
+        pltpu.make_async_copy(source, rollout.at[b, :, lanes], sems.at[4]).start()
+
+    def group(g, carry):
+        for b in range(NB):
+            slot = plan[b]
+            for a in range(4):
+                start(parts.at[slot, 4 * g + a], b, 7 * g + 2 * a)
+        for b in range(NB):
+            slot = plan[b]
+            for a in range(3):
+                start(whole.at[slot, 3 * g + a], b, 7 * g + 2 * a + 1)
+        return carry
+
+    lax.fori_loop(0, 8, group, 0)
+    for copy in states:
         copy.wait()
+    pltpu.make_async_copy(whole, whole, sems.at[4]).wait()
+    pltpu.make_async_copy(parts, parts, sems.at[4]).wait()
 
 
 def body(grad_parts, master, moment, variance, plan, step):
@@ -447,9 +460,9 @@
     dma = pltpu.SemaphoreType.DMA
     results = pl.pallas_call(
         main_kernel,
-        out_shape=outs,
+        out_shape=outs[:3] + [jax.ShapeDtypeStruct((NB, SHARDS, WIDE, LANE), BF16), jax.ShapeDtypeStruct((NB, MERGED, WIDE, LANE), BF16)],
         in_specs=[hbm] * 6,
-        out_specs=[vmem] * 4,
+        out_specs=[vmem] * 5,
         scratch_shapes=[
             pltpu.SMEM((NB,), jnp.int32),
             pltpu.SMEM((NB,), jnp.int32),
@@ -465,8 +478,6 @@
             pltpu.VMEM((ROWS, COLS), BF16),
             pltpu.VMEM((ROWS, COLS), BF16),
             pltpu.VMEM((2, COLS, LANE), BF16),
-            pltpu.VMEM((NB, SHARDS, WIDE, LANE), BF16),
-            pltpu.VMEM((NB, MERGED, WIDE, LANE), BF16),
             pltpu.VMEM((SHARDS, WIDE, LANE), BF16),
             dma((7,)),
             pltpu.SemaphoreType.REGULAR((5,)),
@@ -489,12 +500,12 @@
     new_master, new_moment, new_variance, rollout = pl.pallas_call(
         write_kernel,
         out_shape=outs,
-        in_specs=[vmem] * 4,
+        in_specs=[hbm] + [vmem] * 5,
         out_specs=[hbm] * 4,
-        scratch_shapes=[dma((4,))],
+        scratch_shapes=[pltpu.SMEM((NB,), jnp.int32), dma, dma((5,))],
         compiler_params=pltpu.CompilerParams(vmem_limit_bytes=16 << 20),
         name="write_results",
-    )(*results)
+    )(pltpu.with_memory_space_constraint(plan, pltpu.HBM), *results)
     return (new_master[None], new_moment[None], new_variance[None], rollout)
 
 

time: 72.1 us -> 71.4 us (level)
  no operation moved by 1% of the time
where the time goes in v4:
time: 71.4 us; the launch traced here: 71.3 us
  Pallas kernels  70.6 us (99%)
    pallas_call x1, Pallas kernels, body(): pl.pallas_call(main_kernel, out_shape=outs[:3] + [jax.ShapeDtypeStruct((N...  67.1 us
    pallas_call x1, Pallas kernels, body(): pl.pallas_call(write_kernel, out_shape=outs, in_specs=[hbm] + [vmem] * 5,...  3.53 us

profile of v4, /device:TPU:1, one launch (start us, length us, event | category | flops | bytes accessed | tf_op | source)
XLA Modules:
  0.0 71.3 jit_solution(1090676465683678855)
XLA Ops:
  0.6 67.1 %update_and_hand_off.1 = (f32[224,2048]{1,0:T(8,128)S(1)}, f32[224,2048]{1,0:T(8,128)S(1)}, f32[224,2048]{1,0:T(8,128)S(1)}, bf16[4,32,64,128]{3,2,1,0:T(8,128)(2,1)S(1)}, bf16[4,24,64,128]{3,2,1,0:T(8,128)(2,1)S(1)}) custom-call(s32[4]{0:T(128)} %plan_hbm.3, s32[4]{0:T(128)} %step_hbm.1, bf16[4,224,2048]{2,1,0:T(8,128)(2,1)} %bitcast.7, ...), custom_call_target="tpu_custom_call" | custom-call | tf_op jit(solution)/shard_map/update_and_hand_off/pallas_call | solution.py:461
  67.7 3.5 %write_results.1 = (f32[224,2048]{1,0:T(8,128)}, f32[224,2048]{1,0:T(8,128)}, f32[224,2048]{1,0:T(8,128)}, bf16[4,64,7168]{2,1,0:T(8,128)(2,1)}) custom-call(s32[4]{0:T(128)} %plan_hbm.3, f32[224,2048]{1,0:T(8,128)S(1)} %get-tuple-element.13.master_in, f32[224,2048]{1,0:T(8,128)S(1)} %get-tuple-element.14.moment_in, ...), custom_call_target="tpu_custom_call" | custom-call | tf_op jit(solution)/shard_map/write_results/pallas_call | solution.py:500
